TPU v7x, 32 devices: a whole 2x2x4 slice. The times are simulated.
32 devices in a mesh: row: 4 (over x, core), col: 8 (over z, y).
Axes of the slice: x: 2, y: 2, z: 4, core: 2. Of those that a mesh axis runs over, the one named last changes fastest.
Arguments:
- tile_list: int32 [512, 2], P(('row', 'col')), may hold values from -1 to 63, as said below
- tile_values: bfloat16 [512, 512, 512], P(('row', 'col'))
- block_order: int32 [64], replicated, may hold values from 0 to 63, as said below
- basis: bfloat16 [64, 512, 256], P(('row', 'col')), may hold values from -8 to 8
Outputs:
- basis_out: bfloat16 [64, 512, 256], P(('row', 'col'))
- projected: float32 [256, 256], replicated
Inputs may be any that keep to these rules, and one draw needn't show every extreme that they name: `block_order`: A permutation of the channel blocks; slot p lies on device p // 2 in row-major order of (row, col). `tile_list`: slots of device (i, j) hold tiles whose row block sits in a slot of a device of row index i and whose column block sits in a slot of a device of column index j; each unordered pair of blocks appears at most once in all; empty slots hold -1 in both columns and may stand anywhere among a device's slots; every device holds at most 16 tiles and some device holds exactly 16.
All inputs are finite; a program needn't handle non-finite values.
Results may differ from a plain program's by a relative error of at most 0.0017.
Values may be sent and summed in bfloat16 or wider, within the bound.
A program may use at most 128 MiB of HBM per device.

v0:
```python
import jax
import jax.numpy as jnp
from jax import lax
from jax.sharding import PartitionSpec as P


def per_device(tile_list, tile_values, block_order, basis):
    rows_count = lax.axis_size("row")
    cols_count = lax.axis_size("col")
    own_blocks = basis.shape[0]
    edge = basis.shape[1]
    rank = basis.shape[2]
    blocks_all = block_order.shape[0]
    scale = jnp.sqrt(jnp.float32(blocks_all * edge))
    row_here = lax.axis_index("row")
    row_group = own_blocks * cols_count
    col_group = own_blocks * rows_count
    present = tile_list[:, 0] >= 0
    slot_range = jnp.arange(blocks_all, dtype=jnp.int32)
    ids_both = jnp.where(present[:, None], tile_list, 0)
    match = block_order[None, None, :] == ids_both[:, :, None]
    slots_both = jnp.sum(jnp.where(match, slot_range[None, None, :], 0), axis=2)
    first_slot = slots_both[:, 0]
    second_slot = slots_both[:, 1]
    row_local = jnp.where(present, first_slot - row_here * row_group, row_group)
    owner_second = second_slot // own_blocks
    col_local = jnp.where(
        present, owner_second // cols_count * own_blocks + second_slot % own_blocks, col_group
    )
    column_side = lax.all_gather(basis, "row", axis=0, tiled=True)
    row_side = lax.all_gather(basis, "col", axis=0, tiled=True)
    empty_block = jnp.zeros((1, edge, rank), basis.dtype)
    column_padded = jnp.concatenate([column_side, empty_block], axis=0)
    row_padded = jnp.concatenate([row_side, empty_block], axis=0)
    picked_col = column_padded[col_local]
    picked_row = row_padded[row_local]
    near_prod = jnp.einsum(
        "tab,tbk->tak", tile_values, picked_col, preferred_element_type=jnp.float32
    )
    far_prod = jnp.einsum(
        "tba,tbk->tak", tile_values, picked_row, preferred_element_type=jnp.float32
    )
    col_partial = (
        jnp.zeros((col_group, edge, rank), jnp.float32).at[col_local].add(far_prod, mode="drop")
    )
    row_partial = (
        jnp.zeros((row_group, edge, rank), jnp.float32).at[row_local].add(near_prod, mode="drop")
    )
    row_owned = lax.psum_scatter(row_partial, "col", scatter_dimension=0, tiled=True)
    upper_part = lax.optimization_barrier(col_partial.astype(jnp.bfloat16))
    remainder = col_partial - upper_part.astype(jnp.float32)
    middle_part = lax.optimization_barrier(remainder.astype(jnp.bfloat16))
    lower_part = (remainder - middle_part.astype(jnp.float32)).astype(jnp.bfloat16)
    pieces = jnp.concatenate([upper_part, middle_part, lower_part], axis=2)
    folded = jnp.einsum("sak,saj->kj", column_side, pieces, preferred_element_type=jnp.float32)
    tile_form = folded[:, :rank] + folded[:, rank : 2 * rank] + folded[:, 2 * rank :]
    projected = lax.psum((tile_form + tile_form.T) / scale, ("row", "col"))
    col_owned = lax.psum_scatter(col_partial, "row", scatter_dimension=0, tiled=True)
    product = (row_owned + col_owned).reshape(own_blocks * edge, rank)
    gram_term = jnp.dot(product.T, product, precision=lax.Precision.HIGHEST)
    gram = lax.psum(gram_term, ("row", "col"))
    first_factor = jnp.linalg.cholesky(gram)
    first_basis = lax.linalg.triangular_solve(
        first_factor, product, left_side=False, lower=True, transpose_a=True
    )
    second_term = jnp.dot(first_basis.T, first_basis, precision=lax.Precision.HIGHEST)
    second = lax.psum(second_term, ("row", "col"))
    second_factor = jnp.linalg.cholesky(second)
    final = lax.linalg.triangular_solve(
        second_factor, first_basis, left_side=False, lower=True, transpose_a=True
    )
    basis_out = (final * scale).astype(jnp.bfloat16).reshape(own_blocks, edge, rank)
    return (basis_out, projected)


def solution(mesh):
    in_specs = (
        P(("row", "col"), None),
        P(("row", "col"), None, None),
        P(),
        P(("row", "col"), None, None),
    )
    out_specs = (P(("row", "col"), None, None), P())
    return jax.shard_map(
        per_device, mesh=mesh, in_specs=in_specs, out_specs=out_specs, check_vma=False
    )
```

profile of v0, /device:TPU:1, one launch (start us, length us, event | category | flops | bytes accessed | tf_op | source)
XLA Modules:
  0.0 727.3 jit_solution(8188007919640402378)
XLA Ops:
  11.6 72.2 %all-gather.5.cloned.1.call-done = bf16[16,512,256]{2,1,0:T(8,128)(2,1)} async-done(((bf16[2,512,256]{2,1,0:T(8,128)(2,1)}), bf16[16,512,256]{2,1,0:T(8,128)(2,1)}) %all-gather.5.cloned.1.call-update) | async-done | bytes 4194320 | tf_op jit(solution)/shard_map/all_gather | solution.py:31
  83.8 4.6 concatenate.13
  88.4 5.0 gather_fusion.1
  93.4 10.3 %convolution_bitcast_fusion = f32[16,512,256]{1,2,0:T(8,128)} fusion(bf16[16,512,256]{2,1,0:T(8,128)(2,1)} %gather_fusion.1, bf16[16,512,512]{2,1,0:T(8,128)(2,1)} %param.8), kind=kOutput, calls=%fused_computation.16 | convolution fusion | flops 2147483648 | bytes 20971520 | tf_op jit(solution)/shard_map/tba,tbk->tak/dot_general | solution.py:40
  103.7 9.3 %copy.39 = f32[16,512,256]{2,1,0:T(8,128)} copy(f32[16,512,256]{1,2,0:T(8,128)} %convolution_bitcast_fusion) | data formatting | bytes 16777216 | tf_op jit(solution)/shard_map/tba,tbk->tak/dot_general | solution.py:40
  113.0 2.3 broadcast_in_dim.54
  115.3 16.3 %scatter_fusion.1 = f32[8,512,256]{2,1,0:T(8,128)} fusion(f32[8,512,256]{2,1,0:T(8,128)} %broadcast_in_dim.54, s32[16]{0:T(128)S(1)} %get-tuple-element.46, f32[16,512,256]{2,1,0:T(8,128)} %copy.39), kind=kCustom, calls=%fused_computation.3 | custom fusion | flops 2097152 | bytes 25165888 | tf_op jit(solution)/shard_map/scatter-add | solution.py:44
  131.8 1.7 concatenate.12
  133.5 2.7 gather_fusion
  136.3 11.6 %convolution_bitcast_fusion.1 = f32[16,512,256]{1,2,0:T(8,128)} fusion(bf16[16,512,256]{2,1,0:T(8,128)(2,1)} %gather_fusion, bf16[16,512,512]{2,1,0:T(8,128)(2,1)} %param.8), kind=kOutput, calls=%fused_computation.17 | convolution fusion | flops 2147483648 | bytes 20971520 | tf_op jit(solution)/shard_map/tab,tbk->tak/dot_general | solution.py:37
  147.9 9.4 %copy.37 = f32[16,512,256]{2,1,0:T(8,128)} copy(f32[16,512,256]{1,2,0:T(8,128)} %convolution_bitcast_fusion.1) | data formatting | bytes 16777216 | tf_op jit(solution)/shard_map/tab,tbk->tak/dot_general | solution.py:37
  157.3 4.1 broadcast_in_dim.47
  161.4 16.9 %scatter_fusion = f32[16,512,256]{2,1,0:T(8,128)} fusion(f32[16,512,256]{2,1,0:T(8,128)} %broadcast_in_dim.47, s32[16]{0:T(128)S(1)} %fusion.37, f32[16,512,256]{2,1,0:T(8,128)} %copy.37), kind=kCustom, calls=%fused_computation.2 | custom fusion | flops 2097152 | bytes 25165888 | tf_op jit(solution)/shard_map/scatter-add | solution.py:47
  178.3 12.8 %all-reduce.7.cloned.1.call-start = ((), (), s32[]{:S(2)}) async-start(), calls=%async_computation.6 | async-start | bytes 524288 | tf_op jit(solution)/shard_map/psum | solution.py:61
  191.1 5.4 copy.46
  196.5 2.7 convert_element_type.19
  202.4 1.8 fusion.7
  204.4 123.6 %reduce-scatter.3.cloned.1.call-done = f32[2,512,256]{2,1,0:T(8,128)} async-done(((f32[16,512,256]{2,1,0:T(8,128)}), f32[2,512,256]{2,1,0:T(8,128)}) %reduce-scatter.3.cloned.1.call-update) | async-done | bytes 1048592 | tf_op jit(solution)/shard_map/reduce_scatter | solution.py:49
  329.7 2.5 convolution_bitcast_fusion.2
  333.1 126.2 %all-reduce.7.cloned.1.call-done = f32[256,256]{0,1:T(8,128)} async-done(((f32[256,256]{0,1:T(8,128)}), f32[256,256]{0,1:T(8,128)}) %all-reduce.7.cloned.1.call-update) | async-done | bytes 262160 | tf_op jit(solution)/shard_map/psum | solution.py:61
  461.3 11.7 %cholesky.130 = f32[128,128]{1,0:T(8,128)S(1)} custom-call(f32[128,128]{1,0:T(8,128)S(1)} %cholesky.194), custom_call_target="Cholesky" | custom-call | tf_op jit(solution)/shard_map/jit(cholesky)/cholesky | solution.py:62
  473.1 9.8 %custom-call.13 = f32[1,128,128]{1,2,0:T(8,128)S(1)} custom-call(f32[1,128,128]{2,1,0:T(8,128)S(1)} %get-tuple-element.59), custom_call_target="InvertDiagBlocksLowerTriangular" | custom-call | tf_op jit(solution)/shard_map/jit(cholesky)/cholesky | solution.py:62
  483.4 11.7 %cholesky.147 = f32[128,128]{1,0:T(8,128)S(1)} custom-call(f32[128,128]{1,0:T(8,128)S(1)} %convolution_subtract_fusion.3), custom_call_target="Cholesky" | custom-call | tf_op jit(solution)/shard_map/jit(cholesky)/cholesky | solution.py:62
  497.3 4.1 while.4
  501.4 20.0 %custom-call.14 = f32[2,128,128]{1,2,0:T(8,128)S(1)} custom-call(f32[2,128,128]{2,1,0:T(8,128)S(1)} %get-tuple-element.18), custom_call_target="InvertDiagBlocksLowerTriangular" | custom-call | tf_op jit(solution)/shard_map/triangular_solve/custom-call.0 | solution.py:63
  523.7 1.7 fusion.10
  525.4 128.5 %all-reduce.9.cloned.1.call-done = (f32[256,256]{0,1:T(8,128)}, f32[256,256]{0,1:T(8,128)}) async-done(((f32[256,256]{0,1:T(8,128)}, f32[256,256]{0,1:T(8,128)}), (f32[256,256]{0,1:T(8,128)}, f32[256,256]{0,1:T(8,128)})) %all-reduce.9.cloned.1.call-update) | async-done | bytes 524304 | tf_op jit(solution)/shard_map/psum | solution.py:67
  656.1 11.7 %cholesky.164 = f32[128,128]{1,0:T(8,128)S(1)} custom-call(f32[128,128]{1,0:T(8,128)S(1)} %cholesky.197), custom_call_target="Cholesky" | custom-call | tf_op jit(solution)/shard_map/jit(cholesky)/cholesky | solution.py:68
  667.9 9.8 %custom-call.15 = f32[1,128,128]{1,2,0:T(8,128)S(1)} custom-call(f32[1,128,128]{2,1,0:T(8,128)S(1)} %get-tuple-element.55), custom_call_target="InvertDiagBlocksLowerTriangular" | custom-call | tf_op jit(solution)/shard_map/jit(cholesky)/cholesky | solution.py:68
  678.2 11.9 %cholesky.181 = f32[128,128]{1,0:T(8,128)S(1)} custom-call(f32[128,128]{1,0:T(8,128)S(1)} %convolution_subtract_fusion.2), custom_call_target="Cholesky" | custom-call | tf_op jit(solution)/shard_map/jit(cholesky)/cholesky | solution.py:68
  692.7 4.0 while.5
  696.7 19.7 %custom-call.16 = f32[2,128,128]{1,2,0:T(8,128)S(1)} custom-call(f32[2,128,128]{2,1,0:T(8,128)S(1)} %get-tuple-element.19), custom_call_target="InvertDiagBlocksLowerTriangular" | custom-call | tf_op jit(solution)/shard_map/triangular_solve/custom-call.0 | solution.py:69
  (79 shorter events, 31.9 us)
Async XLA Ops:
  7.2 76.6 %all-gather.5.cloned.1.call-start = ((), (), s32[]{:S(2)}) async-start(), calls=%async_computation.4 | async-start | bytes 4718592 | tf_op jit(solution)/shard_map/all_gather | solution.py:31
  7.9 123.9 %all-gather.3.cloned.1.call-start = ((), (), s32[]{:S(2)}) async-start(), calls=%async_computation.2 | async-start | bytes 2621440 | tf_op jit(solution)/shard_map/all_gather | solution.py:30
  8.6 195.7 %reduce-scatter.5.cloned.1.call-start = ((), (), s32[]{:S(2)}) async-start(), calls=%async_computation.5 | async-start | bytes 5242880 | tf_op jit(solution)/shard_map/reduce_scatter | solution.py:58
  131.7 196.3 %reduce-scatter.3.cloned.1.call-start = ((), (), s32[]{:S(2)}) async-start(), calls=%async_computation.3 | async-start | bytes 9437184 | tf_op jit(solution)/shard_map/reduce_scatter | solution.py:49
  178.3 280.9 %all-reduce.7.cloned.1.call-start = ((), (), s32[]{:S(2)}) async-start(), calls=%async_computation.6 | async-start | bytes 524288 | tf_op jit(solution)/shard_map/psum | solution.py:61
  196.5 3.5 copy-start
  200.8 1.6 copy-start.1
  332.2 321.8 %all-reduce.9.cloned.1.call-start = ((), (), s32[]{:S(2)}) async-start(), calls=%async_computation.7 | async-start | bytes 1048576 | tf_op jit(solution)/shard_map/psum | solution.py:67
  677.9 41.5 %copy-start.2 = (f32[256,256]{0,1:T(8,128)S(1)}, f32[256,256]{0,1:T(8,128)}, u32[]{:S(2)}) copy-start(f32[256,256]{0,1:T(8,128)} %get-tuple-element.43) | copy-start | bytes 786436
Sparse Core Ops, SparseCore 0:
  10.1 73.6 all-gather.4
  85.3 22.6 all-gather.2
  131.8 45.1 reduce-scatter.4
  180.4 147.5 reduce-scatter.2
  333.9 125.2 all-reduce.6
  525.6 128.3 all-reduce.8
where the time goes:
time: 737 us; the launch traced here: 727 us
  waiting for transfers between devices  452 us (61%)
  other arithmetic  154 us (21%)
  local copies, waits for them, and re-layouts  58.2 us (8%)
  matrix products  33 us (4%)
  between operations  17.3 us (2%)
  starting transfers between devices  13 us (2%)
    psum x1, waiting for transfers between devices, per_device(): second = lax.psum(second_term, ('row', 'col'))  129 us
    psum x1, waiting for transfers between devices, per_device(): gram = lax.psum(gram_term, ('row', 'col'))  126 us
    reduce_scatter x1, waiting for transfers between devices, per_device(): lax.psum_scatter(row_partial, 'col', scatter_dimension=0, tiled=True)  124 us
    all_gather x1, waiting for transfers between devices, per_device(): row_side = lax.all_gather(basis, 'col', axis=0, tiled=True)  72.2 us
    another operation x7, other arithmetic, per_device(): second_factor = jnp.linalg.cholesky(second)  34.8 us
    another operation x6, other arithmetic, per_device(): first_factor = jnp.linalg.cholesky(gram)  34 us
    another operation x3, other arithmetic, per_device(): lax.linalg.triangular_solve(first_factor, product, left_side=False, lower...  20 us
    another operation x2, other arithmetic, per_device(): lax.linalg.triangular_solve(second_factor, first_basis, left_side=False,...  19.7 us
  transfers between devices with their start and end apart: 6, of which 4 were waited for; matrix products, arithmetic and copies ran while one was open for 15% of the time, Pallas kernels for 0%

commit v1 on v0

v1 whole, which is shorter than its diff:
```python
import functools

import jax
import jax.numpy as jnp
from jax import lax
from jax.experimental import pallas as pl
from jax.experimental.pallas import tpu as pltpu
from jax.sharding import PartitionSpec as P

MESH = pl.DeviceIdType.MESH
HIGHEST = lax.Precision.HIGHEST
VMEM_MAX = 67043328


def tile_kernel(row_local, col_local, tile_ref, col_side, row_side, row_out, col_out):
    t = pl.program_id(0)

    @pl.when(t == 0)
    def _():
        @pl.loop(0, row_out.shape[0])
        def _(i):
            row_out[i] = jnp.zeros(row_out.shape[1:], jnp.float32)

        @pl.loop(0, col_out.shape[0])
        def _(i):
            col_out[i] = jnp.zeros(col_out.shape[1:], jnp.float32)

    r = row_local[t]
    c = col_local[t]

    @pl.when(r >= 0)
    def _():
        tile = tile_ref[0]
        row_out[r] += jnp.dot(tile, col_side[c], preferred_element_type=jnp.float32)
        col_out[c] += lax.dot_general(
            tile, row_side[r], (((0,), (0,)), ((), ())), preferred_element_type=jnp.float32
        )


def tile_products(row_local, col_local, tiles, col_side, row_side):
    count, edge, _ = tiles.shape
    rank = col_side.shape[2]
    rows, cols = row_side.shape[0], col_side.shape[0]

    def whole(n):
        return pl.BlockSpec(
            (n, edge, rank), lambda t, *_: (0, 0, 0), pipeline_mode=pl.Buffered(1)
        )

    return pl.pallas_call(
        tile_kernel,
        grid_spec=pltpu.PrefetchScalarGridSpec(
            num_scalar_prefetch=2,
            grid=(count,),
            in_specs=[
                pl.BlockSpec((1, edge, edge), lambda t, *_: (t, 0, 0)),
                whole(cols),
                whole(rows),
            ],
            out_specs=[whole(rows), whole(cols)],
        ),
        out_shape=[
            jax.ShapeDtypeStruct((rows, edge, rank), jnp.float32),
            jax.ShapeDtypeStruct((cols, edge, rank), jnp.float32),
        ],
        compiler_params=pltpu.CompilerParams(vmem_limit_bytes=VMEM_MAX),
        name="tile_products",
    )(row_local, col_local, tiles, col_side, row_side)


def sum_kernel(nr, nc, x_ref, out_ref, land_row, mid, land_col, send_sem, recv_sem):
    r = lax.axis_index("row")
    c = lax.axis_index("col")

    def row_peer(o):
        return lax.rem(r + o, nr)

    def col_peer(o):
        return lax.rem(c + o, nc)

    barrier = pltpu.get_barrier_semaphore()
    for o in range(1, nr):
        pl.semaphore_signal(barrier, inc=1, device_id=(row_peer(o), c), device_id_type=MESH)
    for o in range(1, nc):
        pl.semaphore_signal(barrier, inc=1, device_id=(r, col_peer(o)), device_id_type=MESH)
    pl.semaphore_wait(barrier, nr + nc - 2)

    def copy(src, dst, sem, device):
        return pltpu.make_async_remote_copy(
            src_ref=src,
            dst_ref=dst,
            send_sem=send_sem.at[sem],
            recv_sem=recv_sem.at[sem],
            device_id=device,
            device_id_type=MESH,
        )

    base = 0
    copies = []
    for o in range(1, nr):
        p = row_peer(o)
        copies.append(copy(x_ref.at[p], land_row.at[o - 1], base + o - 1, (p, c)))
    for k in copies:
        k.start()
    total = x_ref[r]
    for o, k in enumerate(copies):
        k.wait_recv()
        total += land_row[o]
    mid[...] = total
    sent = copies

    base += nr - 1
    copies = []
    for o in range(1, nc):
        p = col_peer(o)
        copies.append(copy(mid.at[p], land_col.at[o - 1], base + o - 1, (r, p)))
    for k in copies:
        k.start()
    total = mid[c]
    for o, k in enumerate(copies):
        k.wait_recv()
        total += land_col[o]
    out_ref[r, c] = total
    sent = sent + copies

    base += nc - 1
    copies = []
    for o in range(1, nc):
        p = col_peer(o)
        copies.append(copy(out_ref.at[r, c], out_ref.at[r, c], base + o - 1, (r, p)))
    for k in copies:
        k.start()
    for k in copies:
        k.wait_recv()
    sent = sent + copies

    base += nc - 1
    copies = []
    for o in range(1, nr):
        p = row_peer(o)
        copies.append(copy(out_ref.at[r], out_ref.at[r], base + o - 1, (p, c)))
    for k in copies:
        k.start()
    for k in copies:
        k.wait_recv()
    for k in sent + copies:
        k.wait_send()


def sum_all(x, collective_id):
    nr, nc = lax.axis_size("row"), lax.axis_size("col")
    rows, rank = x.shape
    part = rows // (nr * nc)
    sems = 2 * (nr + nc - 2)
    y = pl.pallas_call(
        functools.partial(sum_kernel, nr, nc),
        out_shape=jax.ShapeDtypeStruct((nr, nc, part, rank), jnp.float32),
        in_specs=[pl.BlockSpec(memory_space=pltpu.VMEM)],
        out_specs=pl.BlockSpec(memory_space=pltpu.VMEM),
        scratch_shapes=[
            pltpu.VMEM((nr - 1, nc, part, rank), jnp.float32),
            pltpu.VMEM((nc, part, rank), jnp.float32),
            pltpu.VMEM((nc - 1, part, rank), jnp.float32),
            pltpu.SemaphoreType.DMA((sems,)),
            pltpu.SemaphoreType.DMA((sems,)),
        ],
        compiler_params=pltpu.CompilerParams(collective_id=collective_id, has_side_effects=True),
        name="sum_all",
    )(x.reshape(nr, nc, part, rank))
    return y.reshape(rows, rank)


def invert_panel(x):
    n = x.shape[0]
    rows = lax.broadcasted_iota(jnp.int32, (n, n), 0)
    cols = lax.broadcasted_iota(jnp.int32, (n, n), 1)
    pivots = jnp.ones((n, n), jnp.float32)
    for j in range(n):
        column = jnp.broadcast_to(x[:, j : j + 1], (n, n))
        pivot = jnp.broadcast_to(column[j : j + 1, :], (n, n))
        line = jnp.broadcast_to(x[j : j + 1, :], (n, n))
        line = jnp.where(cols == j, 1.0, line)
        pivots = jnp.where(rows == j, pivot, pivots)
        base = jnp.where(cols == j, 0.0, x)
        x = jnp.where(rows > j, base - (column / pivot) * line, x)
    x = jnp.where(rows == cols, 1.0, jnp.where(rows > cols, x, 0.0))
    return x * lax.rsqrt(pivots)


def inverse_kernel(panel, a_ref, out_ref):
    rank = a_ref.shape[0]
    out_ref[...] = a_ref[...]
    for k in range(rank // panel):
        lo, hi = k * panel, (k + 1) * panel
        inv = invert_panel(out_ref[lo:hi, lo:hi])
        out_ref[lo:hi, lo:hi] = inv
        strip = out_ref[lo:hi, :]
        cols = lax.broadcasted_iota(jnp.int32, strip.shape, 1)
        new = jnp.dot(inv, strip, precision=HIGHEST, preferred_element_type=jnp.float32)
        done = jnp.where((cols >= lo) & (cols < hi), strip, new)
        out_ref[lo:hi, :] = jnp.where(cols < hi, done, 0.0)
        if hi < rank:
            out_ref[hi:, lo:hi] = jnp.zeros((rank - hi, panel), jnp.float32)
            out_ref[hi:, :] -= lax.dot_general(
                new,
                done,
                (((0,), (0,)), ((), ())),
                precision=HIGHEST,
                preferred_element_type=jnp.float32,
            )[hi:, :]


def inverse_factor(a):
    return pl.pallas_call(
        functools.partial(inverse_kernel, 32),
        out_shape=jax.ShapeDtypeStruct(a.shape, jnp.float32),
        in_specs=[pl.BlockSpec(memory_space=pltpu.VMEM)],
        out_specs=pl.BlockSpec(memory_space=pltpu.VMEM),
        name="inverse_factor",
    )(a)


def times_transposed(x, m):
    return lax.dot_general(x, m, (((1,), (1,)), ((), ())), precision=HIGHEST)


def gram_of(x, y):
    return lax.dot_general(x, y, (((0,), (0,)), ((), ())), precision=HIGHEST)


def per_device(tile_list, tile_values, block_order, basis):
    rows_count = lax.axis_size("row")
    cols_count = lax.axis_size("col")
    own_blocks, edge, rank = basis.shape
    blocks_all = block_order.shape[0]
    scale = jnp.sqrt(jnp.float32(blocks_all * edge))
    row_here = lax.axis_index("row")
    row_group = own_blocks * cols_count
    present = tile_list[:, 0] >= 0
    slot_range = jnp.arange(blocks_all, dtype=jnp.int32)
    match = block_order[None, None, :] == tile_list[:, :, None]
    slots_both = jnp.sum(jnp.where(match, slot_range[None, None, :], 0), axis=2)
    first_slot = slots_both[:, 0]
    second_slot = slots_both[:, 1]
    row_local = jnp.where(present, first_slot - row_here * row_group, -1)
    owner_second = second_slot // own_blocks
    col_local = jnp.where(
        present, owner_second // cols_count * own_blocks + second_slot % own_blocks, -1
    )
    column_side = lax.all_gather(basis, "row", axis=0, tiled=True)
    row_side = lax.all_gather(basis, "col", axis=0, tiled=True)
    row_partial, col_partial = tile_products(
        row_local, col_local, tile_values, column_side, row_side
    )
    row_owned = lax.psum_scatter(row_partial, "col", scatter_dimension=0, tiled=True)
    col_owned = lax.psum_scatter(col_partial, "row", scatter_dimension=0, tiled=True)
    product = (row_owned + col_owned).reshape(own_blocks * edge, rank)
    old = basis.reshape(own_blocks * edge, rank).astype(jnp.float32)
    sums = sum_all(jnp.concatenate([gram_of(product, product), gram_of(old, product)], 0), 0)
    gram = sums[:rank]
    projected = sums[rank:] / scale
    first_basis = times_transposed(product, inverse_factor(gram))
    second = sum_all(gram_of(first_basis, first_basis), 1)
    final = times_transposed(first_basis, inverse_factor(second))
    basis_out = (final * scale).astype(jnp.bfloat16).reshape(own_blocks, edge, rank)
    return (basis_out, projected)


def solution(mesh):
    in_specs = (
        P(("row", "col"), None),
        P(("row", "col"), None, None),
        P(),
        P(("row", "col"), None, None),
    )
    out_specs = (P(("row", "col"), None, None), P())
    return jax.shard_map(
        per_device, mesh=mesh, in_specs=in_specs, out_specs=out_specs, check_vma=False
    )
```

time: 737 us -> 471 us (0.64); the launches traced: 727 us -> 471 us
  waiting for transfers between devices: 452 us -> 295 us
  other arithmetic: 154 us -> 6.45 us
  Pallas kernels: 0 us -> 146 us
  local copies, waits for them, and re-layouts: 58.2 us -> 0.01 us
  matrix products: 33 us -> 10.1 us
  starting transfers between devices: 13 us -> 0.16 us
    psum x2 -> x0, waiting for transfers between devices: 255 us -> none  [the longest x1 129 us: per_device(): second = lax.psum(second_term, ('row', 'col'))]
    pallas_call x0 -> x5, Pallas kernels: none -> 146 us  [the longest x2 78.4 us: inverse_factor(): pl.pallas_call(functools.partial(inverse_kernel, 32), out_shape=jax.Shape...]
    another operation x18 -> x0, other arithmetic: 108 us -> none  [the longest x7 34.8 us: per_device(): second_factor = jnp.linalg.cholesky(second)]
    reduce_scatter x1, waiting for transfers between devices: 0.02 us -> 44.6 us  [per_device(): lax.psum_scatter(col_partial, 'row', scatter_dimension=0, tiled=True)]
    scatter-add x2 -> x0, other arithmetic: 33.3 us -> none  [the longest x1 16.9 us: per_device(): jnp.zeros((row_group, edge, rank), jnp.float32).at[row_local]]
    reduce_scatter x1, waiting for transfers between devices: 124 us -> 151 us  [per_device(): lax.psum_scatter(row_partial, 'col', scatter_dimension=0, tiled=True)]
    all_gather x1, waiting for transfers between devices: 0.02 us -> 23.8 us  [per_device(): column_side = lax.all_gather(basis, 'row', axis=0, tiled=True)]
    dot_general x2 -> x0, local copies, waits for them, and re-layouts: 18.7 us -> none  [the longest x1 9.41 us: per_device(): jnp.einsum('tab,tbk->tak', tile_values, picked_col, preferred_element_typ...]
  transfers between devices with their start and end apart: 6 -> 4, of which waited for: 4 -> 4; matrix products, arithmetic and copies ran while one was open for 15% -> 0% of each run, Pallas kernels for 0% -> 0%
where the time goes in v1:
time: 471 us
  waiting for transfers between devices  295 us (63%)
  Pallas kernels  146 us (31%)
  between operations  13.8 us (3%)
  matrix products  10.1 us (2%)
  other arithmetic  6.45 us (1%)
    reduce_scatter x1, waiting for transfers between devices, per_device(): lax.psum_scatter(row_partial, 'col', scatter_dimension=0, tiled=True)  151 us
    pallas_call x2, Pallas kernels, inverse_factor(): pl.pallas_call(functools.partial(inverse_kernel, 32), out_shape=jax.Shape...  78.4 us
    all_gather x1, waiting for transfers between devices, per_device(): row_side = lax.all_gather(basis, 'col', axis=0, tiled=True)  73.3 us
    pallas_call x2, Pallas kernels, sum_all(): pl.pallas_call(functools.partial(sum_kernel, nr, nc), out_shape=jax.Shape...  48.3 us
    reduce_scatter x1, waiting for transfers between devices, per_device(): lax.psum_scatter(col_partial, 'row', scatter_dimension=0, tiled=True)  44.6 us
    all_gather x1, waiting for transfers between devices, per_device(): column_side = lax.all_gather(basis, 'row', axis=0, tiled=True)  23.8 us
    pallas_call x1, Pallas kernels, tile_products(): pl.pallas_call(tile_kernel, grid_spec=pltpu.PrefetchScalarGridSpec(num_sc...  19 us
  transfers between devices with their start and end apart: 4, of which 4 were waited for; matrix products, arithmetic and copies ran while one was open for 0% of the time, Pallas kernels for 0%

profile of v1, /device:TPU:1, one launch (start us, length us, event | category | flops | bytes accessed | tf_op | source)
XLA Modules:
  0.0 470.8 jit_solution(8283374120296616148)
XLA Ops:
  7.2 0.0 all-gather.3.cloned.1.call-start
  7.2 0.7 all-gather.3.cloned.1.call-update
  7.9 0.0 all-gather.5.cloned.1.call-start
  7.9 0.7 all-gather.5.cloned.1.call-update
  8.6 0.0 reduce-scatter.5.cloned.1.call-start
  8.7 0.9 select_reduce_fusion
  9.6 1.2 bitcast_select_fusion
  10.8 23.8 %all-gather.3.cloned.1.call-done.col_side = bf16[8,512,256]{2,1,0:T(8,128)(2,1)} async-done(((bf16[2,512,256]{2,1,0:T(8,128)(2,1)}), bf16[8,512,256]{2,1,0:T(8,128)(2,1)}) %all-gather.3.cloned.1.call-update) | async-done | bytes 2097168 | tf_op jit(solution)/shard_map/all_gather | solution.py:250
  34.6 73.3 %all-gather.5.cloned.1.call-done.row_side = bf16[16,512,256]{2,1,0:T(8,128)(2,1)} async-done(((bf16[2,512,256]{2,1,0:T(8,128)(2,1)}), bf16[16,512,256]{2,1,0:T(8,128)(2,1)}) %all-gather.5.cloned.1.call-update) | async-done | bytes 4194320 | tf_op jit(solution)/shard_map/all_gather | solution.py:251
  107.9 19.0 %tile_products.1 = (f32[16,512,256]{2,1,0:T(8,128)}, f32[8,512,256]{2,1,0:T(8,128)}) custom-call(s32[16]{0:T(128)} %get-tuple-element.9.row_local, s32[16]{0:T(128)} %get-tuple-element.8.col_local, bf16[16,512,512]{2,1,0:T(8,128)(2,1)} %tile_ref.1, bf16[8,512,256]{2,1,0:T(8,128)(2,1)} %all-gather.3.cloned.1.call-done.col_side, ...), custom_call_target="tpu_custom_call" | custom-call | tf_op jit(solution)/shard_map/tile_products/pallas_call | solution.py:50
  126.9 0.0 reduce-scatter.5.cloned.1.call-update
  126.9 0.0 reduce-scatter.3.cloned.1.call-start
  127.0 0.0 copy-start
  127.0 0.5 reduce-scatter.3.cloned.1.call-update
  127.5 44.6 %reduce-scatter.5.cloned.1.call-done = f32[2,512,256]{2,1,0:T(8,128)} async-done(((f32[8,512,256]{2,1,0:T(8,128)}), f32[2,512,256]{2,1,0:T(8,128)}) %reduce-scatter.5.cloned.1.call-update) | async-done | bytes 1048592 | tf_op jit(solution)/shard_map/reduce_scatter | solution.py:256
  172.2 150.9 %reduce-scatter.3.cloned.1.call-done = f32[2,512,256]{2,1,0:T(8,128)} async-done(((f32[16,512,256]{2,1,0:T(8,128)}), f32[2,512,256]{2,1,0:T(8,128)}) %reduce-scatter.3.cloned.1.call-update) | async-done | bytes 1048592 | tf_op jit(solution)/shard_map/reduce_scatter | solution.py:255
  323.1 1.7 add.20
  324.7 0.0 copy-done
  324.8 0.8 convolution_bitcast_fusion
  325.6 1.8 convolution_bitcast_fusion.1
  327.4 0.8 pad_maximum_fusion
  328.2 27.2 %sum_all.2 = f32[4,8,16,256]{3,2,1,0:T(8,128)} custom-call(f32[4,8,16,256]{3,2,1,0:T(8,128)} %bitcast.42), custom_call_target="tpu_custom_call" | custom-call | tf_op jit(solution)/shard_map/sum_all/pallas_call | solution.py:155
  355.4 1.9 slice_multiply_fusion
  357.3 39.2 %inverse_factor.2 = f32[256,256]{1,0:T(8,128)} custom-call(f32[256,256]{1,0:T(8,128)} %bitcast.45), custom_call_target="tpu_custom_call" | custom-call | tf_op jit(solution)/shard_map/inverse_factor/pallas_call | solution.py:214
  396.5 2.0 fusion.2
  398.4 2.7 fusion.3
  401.2 21.2 %sum_all.3 = f32[4,8,8,256]{3,2,1,0:T(8,128)} custom-call(f32[4,8,8,256]{3,2,1,0:T(8,128)} %bitcast.43), custom_call_target="tpu_custom_call" | custom-call | tf_op jit(solution)/shard_map/sum_all/pallas_call | solution.py:155
  422.3 39.2 %inverse_factor.3 = f32[256,256]{1,0:T(8,128)} custom-call(f32[256,256]{1,0:T(8,128)} %bitcast.44), custom_call_target="tpu_custom_call" | custom-call | tf_op jit(solution)/shard_map/inverse_factor/pallas_call | solution.py:214
  461.5 2.8 fusion
Async XLA Ops:
  7.2 27.4 %all-gather.3.cloned.1.call-start = ((), (), s32[]{:S(2)}) async-start(), calls=%async_computation.2 | async-start | bytes 2621440 | tf_op jit(solution)/shard_map/all_gather | solution.py:250
  7.9 100.0 %all-gather.5.cloned.1.call-start = ((), (), s32[]{:S(2)}) async-start(), calls=%async_computation.3 | async-start | bytes 4718592 | tf_op jit(solution)/shard_map/all_gather | solution.py:251
  8.6 163.5 %reduce-scatter.5.cloned.1.call-start = ((), (), s32[]{:S(2)}) async-start(), calls=%async_computation.5 | async-start | bytes 5242880 | tf_op jit(solution)/shard_map/reduce_scatter | solution.py:256
  126.9 196.1 %reduce-scatter.3.cloned.1.call-start = ((), (), s32[]{:S(2)}) async-start(), calls=%async_computation.4 | async-start | bytes 9437184 | tf_op jit(solution)/shard_map/reduce_scatter | solution.py:255
  127.0 197.8 %copy-start = (bf16[2,512,256]{2,1,0:T(8,128)(2,1)S(1)}, bf16[2,512,256]{2,1,0:T(8,128)(2,1)}, u32[]{:S(2)}) copy-start(bf16[2,512,256]{2,1,0:T(8,128)(2,1)} %param.7) | copy-start | bytes 1572868
Sparse Core Ops, SparseCore 0:
  9.5 25.0 all-gather.2
  36.7 71.1 all-gather.4
  127.1 45.0 reduce-scatter.4
  175.7 147.3 reduce-scatter.2

commit v2 on v1

--- a/solution.py
+++ b/solution.py
@@ -170,6 +170,237 @@
     return y.reshape(rows, rank)
 
 
+class Side:
+    def __init__(self, axis, count, inner_count):
+        self.axis = axis
+        self.inner_count = inner_count
+        self.outer_count = count // inner_count
+        index = lax.axis_index(axis)
+        self.inner = lax.rem(index, inner_count)
+        self.outer = lax.div(index, inner_count)
+
+    def place(self, outer_step, inner_step):
+        outer = lax.rem(self.outer + outer_step, self.outer_count)
+        inner = lax.rem(self.inner + inner_step, self.inner_count)
+        return outer * self.inner_count + inner
+
+    def device(self, outer_step, inner_step):
+        index = self.place(outer_step, inner_step)
+        if self.axis == "row":
+            return (index, lax.axis_index("col"))
+        return (lax.axis_index("row"), index)
+
+    def peers(self):
+        inner = [(0, t) for t in range(1, self.inner_count)]
+        return inner + [(s, 0) for s in range(1, self.outer_count)]
+
+
+def inner_of(count):
+    inner = 1
+    while inner * inner * 4 <= count:
+        inner *= 2
+    return inner
+
+
+def make_sides(nr, nc):
+    return Side("row", nr, 2), Side("col", nc, inner_of(nc))
+
+
+def greet(sides):
+    barrier = pltpu.get_barrier_semaphore()
+    total = 0
+    for side in sides:
+        for step in side.peers():
+            pl.semaphore_signal(
+                barrier, inc=1, device_id=side.device(*step), device_id_type=MESH
+            )
+            total += 1
+    pl.semaphore_wait(barrier, total)
+
+
+class Sender:
+    def __init__(self, send_sem, recv_sem):
+        self.send_sem, self.recv_sem, self.sent = send_sem, recv_sem, []
+
+    def start(self, src, dst, device):
+        n = len(self.sent)
+        copy = pltpu.make_async_remote_copy(
+            src_ref=src,
+            dst_ref=dst,
+            send_sem=self.send_sem.at[n],
+            recv_sem=self.recv_sem.at[n],
+            device_id=device,
+            device_id_type=MESH,
+        )
+        copy.start()
+        self.sent.append(copy)
+        return copy
+
+    def finish(self):
+        for copy in self.sent:
+            copy.wait_send()
+
+
+def gather_kernel(nr, nc, own, own_ref, col_side, row_side, send_sem, recv_sem, local_sem):
+    sides = make_sides(nr, nc)
+    outs = (col_side, row_side)
+    greet(sides)
+    sender = Sender(send_sem, recv_sem)
+
+    def at(out, index):
+        return out.at[pl.ds(index * own, own)]
+
+    first = []
+    for side, out in zip(sides, outs):
+        mine = at(out, side.place(0, 0))
+        for t in range(1, side.inner_count):
+            first.append(sender.start(own_ref, mine, side.device(0, t)))
+    outer = []
+    for side, out in zip(sides, outs):
+        mine = at(out, side.place(0, 0))
+        for s in range(1, side.outer_count):
+            outer.append((side, out, s, sender.start(own_ref, mine, side.device(s, 0))))
+    local = []
+    for k, (side, out) in enumerate(zip(sides, outs)):
+        copy = pltpu.make_async_copy(own_ref, at(out, side.place(0, 0)), local_sem.at[k])
+        copy.start()
+        local.append(copy)
+    for side, out, s, copy in outer:
+        copy.wait_recv()
+        got = at(out, side.place(side.outer_count - s, 0))
+        for t in range(1, side.inner_count):
+            first.append(sender.start(got, got, side.device(0, t)))
+    for copy in first:
+        copy.wait_recv()
+    for copy in local:
+        copy.wait()
+    sender.finish()
+
+
+def side_copies(count, inner):
+    outer = count // inner
+    return outer - 1 + outer * (inner - 1)
+
+
+def gather_sides(basis):
+    nr, nc = lax.axis_size("row"), lax.axis_size("col")
+    own = basis.shape[0]
+    sems = side_copies(nr, 2) + side_copies(nc, inner_of(nc))
+    return pl.pallas_call(
+        functools.partial(gather_kernel, nr, nc, own),
+        out_shape=[
+            jax.ShapeDtypeStruct((n * own,) + basis.shape[1:], basis.dtype) for n in (nr, nc)
+        ],
+        in_specs=[pl.BlockSpec(memory_space=pltpu.VMEM)],
+        out_specs=[pl.BlockSpec(memory_space=pl.ANY)] * 2,
+        scratch_shapes=[
+            pltpu.SemaphoreType.DMA((sems,)),
+            pltpu.SemaphoreType.DMA((sems,)),
+            pltpu.SemaphoreType.DMA((2,)),
+        ],
+        compiler_params=pltpu.CompilerParams(collective_id=2, has_side_effects=True),
+        name="gather_sides",
+    )(basis)
+
+
+def add_into(dst, src):
+    edge = dst.shape[0]
+    step = min(64, edge)
+
+    @pl.loop(0, edge // step)
+    def _(i):
+        part = pl.ds(pl.multiple_of(i * step, step), step)
+        dst[part, :] += src[part, :]
+
+
+def scatter_kernel(nr, nc, own, col_ref, row_ref, out_ref, *scratch):
+    bufs, (send_sem, recv_sem, local_sem) = scratch[:-3], scratch[-3:]
+    sides = make_sides(nr, nc)
+    greet(sides)
+    sender = Sender(send_sem, recv_sem)
+    local_count = 0
+    plans = []
+    for side, ref, k in ((sides[0], col_ref, 0), (sides[1], row_ref, 3)):
+        mid, land_in, land_out = bufs[k : k + 3]
+        steps = []
+        for s in range(1, side.outer_count + 1):
+            for b in range(own):
+                waits = []
+                for t in range(1, side.inner_count):
+                    waits.append(
+                        sender.start(
+                            ref.at[side.place(s, t) * own + b],
+                            land_in.at[t - 1, s - 1, b],
+                            side.device(0, t),
+                        )
+                    )
+                keep = pltpu.make_async_copy(
+                    ref.at[side.place(s, 0) * own + b], mid.at[s - 1, b], local_sem.at[local_count]
+                )
+                keep.start()
+                local_count += 1
+                steps.append((s, b, waits, keep))
+        plans.append((side, mid, land_in, land_out, steps))
+    arrivals = []
+    for side, mid, land_in, land_out, steps in plans:
+        for s, b, waits, keep in steps:
+            keep.wait()
+            for t, copy in enumerate(waits):
+                copy.wait_recv()
+                add_into(mid.at[s - 1, b], land_in.at[t, s - 1, b])
+            if s < side.outer_count:
+                copy = sender.start(
+                    mid.at[s - 1, b], land_out.at[s - 1, b], side.device(s, 0)
+                )
+                arrivals.append((mid, land_out, s, b, side, copy))
+    for mid, land_out, s, b, side, copy in arrivals:
+        copy.wait_recv()
+        add_into(mid.at[side.outer_count - 1, b], land_out.at[s - 1, b])
+    col_mid, row_mid = plans[0][1], plans[1][1]
+    col_last, row_last = plans[0][0].outer_count - 1, plans[1][0].outer_count - 1
+    edge = out_ref.shape[1]
+    step = min(64, edge)
+    for b in range(own):
+
+        @pl.loop(0, edge // step)
+        def _(i):
+            part = pl.ds(pl.multiple_of(i * step, step), step)
+            out_ref[b, part, :] = col_mid[col_last, b, part, :] + row_mid[row_last, b, part, :]
+
+    sender.finish()
+
+
+def scatter_sums(col_partial, row_partial, own):
+    nr, nc = lax.axis_size("row"), lax.axis_size("col")
+    block = col_partial.shape[1:]
+    scratch = []
+    for count, inner in ((nr, 2), (nc, inner_of(nc))):
+        outer = count // inner
+        scratch += [
+            pltpu.VMEM((outer, own) + block, jnp.float32),
+            pltpu.VMEM((max(inner - 1, 1), outer, own) + block, jnp.float32),
+            pltpu.VMEM((max(outer - 1, 1), own) + block, jnp.float32),
+        ]
+    sems = own * (side_copies(nr, 2) + side_copies(nc, inner_of(nc)))
+    locals_ = own * (nr // 2 + nc // inner_of(nc))
+    return pl.pallas_call(
+        functools.partial(scatter_kernel, nr, nc, own),
+        out_shape=jax.ShapeDtypeStruct((own,) + block, jnp.float32),
+        in_specs=[pl.BlockSpec(memory_space=pl.ANY)] * 2,
+        out_specs=pl.BlockSpec(memory_space=pltpu.VMEM),
+        scratch_shapes=scratch
+        + [
+            pltpu.SemaphoreType.DMA((sems,)),
+            pltpu.SemaphoreType.DMA((sems,)),
+            pltpu.SemaphoreType.DMA((locals_,)),
+        ],
+        compiler_params=pltpu.CompilerParams(
+            collective_id=3, has_side_effects=True, vmem_limit_bytes=VMEM_MAX
+        ),
+        name="scatter_sums",
+    )(col_partial, row_partial)
+
+
 def invert_panel(x):
     n = x.shape[0]
     rows = lax.broadcasted_iota(jnp.int32, (n, n), 0)
@@ -177,12 +408,12 @@
     pivots = jnp.ones((n, n), jnp.float32)
     for j in range(n):
         column = jnp.broadcast_to(x[:, j : j + 1], (n, n))
-        pivot = jnp.broadcast_to(column[j : j + 1, :], (n, n))
-        line = jnp.broadcast_to(x[j : j + 1, :], (n, n))
-        line = jnp.where(cols == j, 1.0, line)
-        pivots = jnp.where(rows == j, pivot, pivots)
+        pivot = column[j : j + 1, :]
+        line = jnp.where(cols[j : j + 1, :] == j, 1.0, x[j : j + 1, :]) / pivot
+        pivots = jnp.where(rows == j, column, pivots)
         base = jnp.where(cols == j, 0.0, x)
-        x = jnp.where(rows > j, base - (column / pivot) * line, x)
+        x = base - jnp.where(rows > j, column, 0.0) * jnp.broadcast_to(line, (n, n))
+        x = jnp.where((cols == j) & (rows == j), 1.0, x)
     x = jnp.where(rows == cols, 1.0, jnp.where(rows > cols, x, 0.0))
     return x * lax.rsqrt(pivots)
 
@@ -247,14 +478,11 @@
     col_local = jnp.where(
         present, owner_second // cols_count * own_blocks + second_slot % own_blocks, -1
     )
-    column_side = lax.all_gather(basis, "row", axis=0, tiled=True)
-    row_side = lax.all_gather(basis, "col", axis=0, tiled=True)
+    column_side, row_side = gather_sides(basis)
     row_partial, col_partial = tile_products(
         row_local, col_local, tile_values, column_side, row_side
     )
-    row_owned = lax.psum_scatter(row_partial, "col", scatter_dimension=0, tiled=True)
-    col_owned = lax.psum_scatter(col_partial, "row", scatter_dimension=0, tiled=True)
-    product = (row_owned + col_owned).reshape(own_blocks * edge, rank)
+    product = scatter_sums(col_partial, row_partial, own_blocks).reshape(own_blocks * edge, rank)
     old = basis.reshape(own_blocks * edge, rank).astype(jnp.float32)
     sums = sum_all(jnp.concatenate([gram_of(product, product), gram_of(old, product)], 0), 0)
     gram = sums[:rank]

time: 471 us -> 326 us (0.69)
  waiting for transfers between devices: 295 us -> 0 us
  Pallas kernels: 146 us -> 306 us
  between operations: 13.8 us -> 0.7 us
    reduce_scatter x2 -> x0, waiting for transfers between devices: 196 us -> none  [the longest x1 151 us: per_device(): lax.psum_scatter(row_partial, 'col', scatter_dimension=0, tiled=True)]
    pallas_call x0 -> x2, Pallas kernels: none -> 177 us  [the longest x1 114 us: scatter_sums(): pl.pallas_call(functools.partial(scatter_kernel, nr, nc, own), out_shape=...]
    all_gather x2 -> x0, waiting for transfers between devices: 97.2 us -> none  [the longest x1 73.3 us: per_device(): row_side = lax.all_gather(basis, 'col', axis=0, tiled=True)]
    pallas_call x2, Pallas kernels: 78.4 us -> 56.2 us  [inverse_factor(): pl.pallas_call(functools.partial(inverse_kernel, 32), out_shape=jax.Shape...]
    pallas_call x2, Pallas kernels: 48.3 us -> 54.6 us  [sum_all(): pl.pallas_call(functools.partial(sum_kernel, nr, nc), out_shape=jax.Shape...]
  transfers between devices with their start and end apart: 4 -> 0, of which waited for: 4 -> 0; matrix products, arithmetic and copies ran while one was open for 0% -> 0% of each run, Pallas kernels for 0% -> 0%
where the time goes in v2:
time: 326 us; the launch traced here: 325 us
  Pallas kernels  306 us (94%)
  matrix products  13 us (4%)
  other arithmetic  4.77 us (1%)
    pallas_call x1, Pallas kernels, scatter_sums(): pl.pallas_call(functools.partial(scatter_kernel, nr, nc, own), out_shape=...  114 us
    pallas_call x1, Pallas kernels, gather_sides(): pl.pallas_call(functools.partial(gather_kernel, nr, nc, own), out_shape=[...  62.4 us
    pallas_call x2, Pallas kernels, inverse_factor(): pl.pallas_call(functools.partial(inverse_kernel, 32), out_shape=jax.Shape...  56.2 us
    pallas_call x2, Pallas kernels, sum_all(): pl.pallas_call(functools.partial(sum_kernel, nr, nc), out_shape=jax.Shape...  54.6 us
    pallas_call x1, Pallas kernels, tile_products(): pl.pallas_call(tile_kernel, grid_spec=pltpu.PrefetchScalarGridSpec(num_sc...  19 us
    dot_general x3, matrix products, gram_of(): return lax.dot_general(x, y, (((0,), (0,)), ((), ())), precision=HIGHEST)  8.22 us

profile of v2, /device:TPU:1, one launch (start us, length us, event | category | flops | bytes accessed | tf_op | source)
XLA Modules:
  0.0 324.8 jit_solution(3836854328043918401)
XLA Ops:
  0.6 0.9 select_reduce_fusion
  1.5 1.2 bitcast_select_fusion
  2.7 62.4 %gather_sides.1 = (bf16[8,512,256]{2,1,0:T(8,128)(2,1)}, bf16[16,512,256]{2,1,0:T(8,128)(2,1)}) custom-call(bf16[2,512,256]{2,1,0:T(8,128)(2,1)} %own_ref.1), custom_call_target="tpu_custom_call" | custom-call | tf_op jit(solution)/shard_map/gather_sides/pallas_call | solution.py:289
  65.1 19.0 %tile_products.1 = (f32[16,512,256]{2,1,0:T(8,128)}, f32[8,512,256]{2,1,0:T(8,128)}) custom-call(s32[16]{0:T(128)} %get-tuple-element.13.row_local, s32[16]{0:T(128)} %get-tuple-element.12.col_local, bf16[16,512,512]{2,1,0:T(8,128)(2,1)} %tile_ref.1, bf16[8,512,256]{2,1,0:T(8,128)(2,1)} %get-tuple-element.6.col_side, ...), custom_call_target="tpu_custom_call" | custom-call | tf_op jit(solution)/shard_map/tile_products/pallas_call | solution.py:50
  84.1 114.2 %scatter_sums.1 = f32[2,512,256]{2,1,0:T(8,128)} custom-call(f32[8,512,256]{2,1,0:T(8,128)} %get-tuple-element.8.col_ref, f32[16,512,256]{2,1,0:T(8,128)} %get-tuple-element.9.row_ref), custom_call_target="tpu_custom_call" | custom-call | tf_op jit(solution)/shard_map/scatter_sums/pallas_call | solution.py:386
  198.3 0.0 copy-start
  198.3 2.2 convolution_bitcast_fusion
  200.6 3.5 %convolution_bitcast_fusion.1 = f32[256,256]{1,0:T(8,128)S(1)} fusion(f32[2,512,256]{2,1,0:T(8,128)} %scatter_sums.1), kind=kOutput, calls=%fused_computation.3 | convolution fusion | flops 805306368 | bytes 1310720 | tf_op jit(solution)/shard_map/dot_general | solution.py:459
  204.0 0.8 pad_maximum_fusion
  204.9 34.1 %sum_all.2 = f32[4,8,16,256]{3,2,1,0:T(8,128)} custom-call(f32[4,8,16,256]{3,2,1,0:T(8,128)} %bitcast.42), custom_call_target="tpu_custom_call" | custom-call | tf_op jit(solution)/shard_map/sum_all/pallas_call | solution.py:155
  239.0 1.9 slice_multiply_fusion
  240.8 28.1 %inverse_factor.2 = f32[256,256]{1,0:T(8,128)} custom-call(f32[256,256]{1,0:T(8,128)} %bitcast.45), custom_call_target="tpu_custom_call" | custom-call | tf_op jit(solution)/shard_map/inverse_factor/pallas_call | solution.py:445
  268.9 0.0 copy-done
  268.9 2.0 fusion.2
  270.9 2.5 fusion.3
  273.4 20.5 %sum_all.3 = f32[4,8,8,256]{3,2,1,0:T(8,128)} custom-call(f32[4,8,8,256]{3,2,1,0:T(8,128)} %bitcast.43), custom_call_target="tpu_custom_call" | custom-call | tf_op jit(solution)/shard_map/sum_all/pallas_call | solution.py:155
  293.9 28.1 %inverse_factor.3 = f32[256,256]{1,0:T(8,128)} custom-call(f32[256,256]{1,0:T(8,128)} %bitcast.44), custom_call_target="tpu_custom_call" | custom-call | tf_op jit(solution)/shard_map/inverse_factor/pallas_call | solution.py:445
  322.0 2.8 fusion
Async XLA Ops:
  198.3 70.6 %copy-start = (f32[2,512,256]{2,1,0:T(8,128)S(1)}, f32[2,512,256]{2,1,0:T(8,128)}, u32[]{:S(2)}) copy-start(f32[2,512,256]{2,1,0:T(8,128)} %scatter_sums.1) | copy-start | bytes 3145732

commit v3 on v2

--- a/solution.py
+++ b/solution.py
@@ -246,28 +246,24 @@
     outs = (col_side, row_side)
     greet(sides)
     sender = Sender(send_sem, recv_sem)
-
-    def at(out, index):
-        return out.at[pl.ds(index * own, own)]
-
-    first = []
-    for side, out in zip(sides, outs):
-        mine = at(out, side.place(0, 0))
+    first, outer, local = [], [], []
+    for k, (side, out) in reversed(list(enumerate(zip(sides, outs)))):
+        mine = side.place(0, 0) * own
+        for s in range(1, side.outer_count):
+            for b in range(own):
+                copy = sender.start(own_ref.at[b], out.at[mine + b], side.device(s, 0))
+                outer.append((side, out, s, b, copy))
         for t in range(1, side.inner_count):
-            first.append(sender.start(own_ref, mine, side.device(0, t)))
-    outer = []
-    for side, out in zip(sides, outs):
-        mine = at(out, side.place(0, 0))
-        for s in range(1, side.outer_count):
-            outer.append((side, out, s, sender.start(own_ref, mine, side.device(s, 0))))
-    local = []
-    for k, (side, out) in enumerate(zip(sides, outs)):
-        copy = pltpu.make_async_copy(own_ref, at(out, side.place(0, 0)), local_sem.at[k])
+            for b in range(own):
+                first.append(
+                    sender.start(own_ref.at[b], out.at[mine + b], side.device(0, t))
+                )
+        copy = pltpu.make_async_copy(own_ref, out.at[pl.ds(mine, own)], local_sem.at[k])
         copy.start()
         local.append(copy)
-    for side, out, s, copy in outer:
+    for side, out, s, b, copy in outer:
         copy.wait_recv()
-        got = at(out, side.place(side.outer_count - s, 0))
+        got = out.at[side.place(side.outer_count - s, 0) * own + b]
         for t in range(1, side.inner_count):
             first.append(sender.start(got, got, side.device(0, t)))
     for copy in first:
@@ -285,7 +281,7 @@
 def gather_sides(basis):
     nr, nc = lax.axis_size("row"), lax.axis_size("col")
     own = basis.shape[0]
-    sems = side_copies(nr, 2) + side_copies(nc, inner_of(nc))
+    sems = own * (side_copies(nr, 2) + side_copies(nc, inner_of(nc)))
     return pl.pallas_call(
         functools.partial(gather_kernel, nr, nc, own),
         out_shape=[
@@ -323,7 +319,8 @@
     for side, ref, k in ((sides[0], col_ref, 0), (sides[1], row_ref, 3)):
         mid, land_in, land_out = bufs[k : k + 3]
         steps = []
-        for s in range(1, side.outer_count + 1):
+        middle = side.outer_count // 2
+        for s in sorted(range(1, side.outer_count + 1), key=lambda s: (s != middle, s)):
             for b in range(own):
                 waits = []
                 for t in range(1, side.inner_count):
@@ -406,19 +403,27 @@
     rows = lax.broadcasted_iota(jnp.int32, (n, n), 0)
     cols = lax.broadcasted_iota(jnp.int32, (n, n), 1)
     pivots = jnp.ones((n, n), jnp.float32)
-    for j in range(n):
-        column = jnp.broadcast_to(x[:, j : j + 1], (n, n))
-        pivot = column[j : j + 1, :]
-        line = jnp.where(cols[j : j + 1, :] == j, 1.0, x[j : j + 1, :]) / pivot
-        pivots = jnp.where(rows == j, column, pivots)
-        base = jnp.where(cols == j, 0.0, x)
-        x = base - jnp.where(rows > j, column, 0.0) * jnp.broadcast_to(line, (n, n))
-        x = jnp.where((cols == j) & (rows == j), 1.0, x)
+    group = 4
+    for start in range(0, n, group):
+        members = range(start, start + group)
+        columns = {j: jnp.broadcast_to(x[:, j : j + 1], (n, n)) for j in members}
+        for j in members:
+            column = columns[j]
+            pivot = column[j : j + 1, :]
+            inverse = 1.0 / pivot
+            below = jnp.where(rows > j, column, 0.0)
+            for k in range(j + 1, start + group):
+                factor = columns[k][j : j + 1, :] * inverse
+                columns[k] = columns[k] - below * jnp.broadcast_to(factor, (n, n))
+            line = jnp.where(cols[j : j + 1, :] == j, 1.0, x[j : j + 1, :]) * inverse
+            pivots = jnp.where(rows == j, column, pivots)
+            base = jnp.where(cols == j, jnp.where(rows == j, 1.0, 0.0), x)
+            x = base - below * jnp.broadcast_to(line, (n, n))
     x = jnp.where(rows == cols, 1.0, jnp.where(rows > cols, x, 0.0))
     return x * lax.rsqrt(pivots)
 
 
-def inverse_kernel(panel, a_ref, out_ref):
+def eliminate(panel, a_ref, out_ref):
     rank = a_ref.shape[0]
     out_ref[...] = a_ref[...]
     for k in range(rank // panel):
@@ -441,9 +446,55 @@
             )[hi:, :]
 
 
-def inverse_factor(a):
+def inverse_kernel(panel, near_identity, a_ref, out_ref):
+    if not near_identity:
+        eliminate(panel, a_ref, out_ref)
+        return
+    rows = lax.broadcasted_iota(jnp.int32, a_ref.shape, 0)
+    cols = lax.broadcasted_iota(jnp.int32, a_ref.shape, 1)
+    unit = jnp.where(rows == cols, 1.0, 0.0)
+
+    def lower_half(e):
+        return jnp.where(rows > cols, e, jnp.where(rows == cols, 0.5 * e, 0.0))
+
+    def dot(x, y, contract):
+        return lax.dot_general(
+            x,
+            y,
+            (((1,), (contract,)), ((), ())),
+            precision=HIGHEST,
+            preferred_element_type=jnp.float32,
+        )
+
+    error = a_ref[...] - unit
+    size = jnp.sum(error * error)
+    near = size < 0.04
+
+    @pl.when(jnp.logical_not(near))
+    def _():
+        eliminate(panel, a_ref, out_ref)
+
+    @pl.when(near)
+    def _():
+        out_ref[...] = unit - lower_half(error)
+
+        def more(carry):
+            step, last = carry
+            return (step < 4) & (last > 1e-9)
+
+        def improve(carry):
+            step, _ = carry
+            w = out_ref[...]
+            e = dot(dot(w, a_ref[...], 0), w, 1) - unit
+            out_ref[...] = w - dot(lower_half(e), w, 0)
+            return step + 1, jnp.sum(e * e)
+
+        lax.while_loop(more, improve, (0, size))
+
+
+def inverse_factor(a, near_identity=False):
     return pl.pallas_call(
-        functools.partial(inverse_kernel, 32),
+        functools.partial(inverse_kernel, 32, near_identity),
         out_shape=jax.ShapeDtypeStruct(a.shape, jnp.float32),
         in_specs=[pl.BlockSpec(memory_space=pltpu.VMEM)],
         out_specs=pl.BlockSpec(memory_space=pltpu.VMEM),
@@ -489,7 +540,7 @@
     projected = sums[rank:] / scale
     first_basis = times_transposed(product, inverse_factor(gram))
     second = sum_all(gram_of(first_basis, first_basis), 1)
-    final = times_transposed(first_basis, inverse_factor(second))
+    final = times_transposed(first_basis, inverse_factor(second, near_identity=True))
     basis_out = (final * scale).astype(jnp.bfloat16).reshape(own_blocks, edge, rank)
     return (basis_out, projected)
 

time: 326 us -> 283 us (0.87)
  Pallas kernels: 306 us -> 263 us
    pallas_call x2, Pallas kernels: 56.2 us -> 19.4 us  [inverse_factor(): pl.pallas_call(functools.partial(inverse_kernel, 32, near_identity), out_...]
    pallas_call x1, Pallas kernels: 62.4 us -> 57 us  [gather_sides(): pl.pallas_call(functools.partial(gather_kernel, nr, nc, own), out_shape=[...]
    pallas_call x1, Pallas kernels: 114 us -> 120 us  [scatter_sums(): pl.pallas_call(functools.partial(scatter_kernel, nr, nc, own), out_shape=...]
    pallas_call x2, Pallas kernels: 54.6 us -> 49.3 us  [sum_all(): pl.pallas_call(functools.partial(sum_kernel, nr, nc), out_shape=jax.Shape...]
where the time goes in v3:
time: 283 us; the launch traced here: 282 us
  Pallas kernels  263 us (93%)
  matrix products  13 us (5%)
  other arithmetic  4.77 us (2%)
    pallas_call x1, Pallas kernels, scatter_sums(): pl.pallas_call(functools.partial(scatter_kernel, nr, nc, own), out_shape=...  120 us
    pallas_call x1, Pallas kernels, gather_sides(): pl.pallas_call(functools.partial(gather_kernel, nr, nc, own), out_shape=[...  57 us
    pallas_call x2, Pallas kernels, sum_all(): pl.pallas_call(functools.partial(sum_kernel, nr, nc), out_shape=jax.Shape...  49.3 us
    pallas_call x2, Pallas kernels, inverse_factor(): pl.pallas_call(functools.partial(inverse_kernel, 32, near_identity), out_...  19.4 us
    pallas_call x1, Pallas kernels, tile_products(): pl.pallas_call(tile_kernel, grid_spec=pltpu.PrefetchScalarGridSpec(num_sc...  18.1 us
    dot_general x3, matrix products, gram_of(): return lax.dot_general(x, y, (((0,), (0,)), ((), ())), precision=HIGHEST)  8.22 us

profile of v3, /device:TPU:1, one launch (start us, length us, event | category | flops | bytes accessed | tf_op | source)
XLA Modules:
  0.0 281.7 jit_solution(11144980570439717687)
XLA Ops:
  0.6 0.9 select_reduce_fusion
  1.5 1.2 bitcast_select_fusion
  2.7 57.0 %gather_sides.1 = (bf16[8,512,256]{2,1,0:T(8,128)(2,1)}, bf16[16,512,256]{2,1,0:T(8,128)(2,1)}) custom-call(bf16[2,512,256]{2,1,0:T(8,128)(2,1)} %own_ref.1), custom_call_target="tpu_custom_call" | custom-call | tf_op jit(solution)/shard_map/gather_sides/pallas_call | solution.py:285
  59.7 18.1 %tile_products.1 = (f32[16,512,256]{2,1,0:T(8,128)}, f32[8,512,256]{2,1,0:T(8,128)}) custom-call(s32[16]{0:T(128)} %get-tuple-element.13.row_local, s32[16]{0:T(128)} %get-tuple-element.12.col_local, bf16[16,512,512]{2,1,0:T(8,128)(2,1)} %tile_ref.1, bf16[8,512,256]{2,1,0:T(8,128)(2,1)} %get-tuple-element.6.col_side, ...), custom_call_target="tpu_custom_call" | custom-call | tf_op jit(solution)/shard_map/tile_products/pallas_call | solution.py:50
  77.8 119.5 %scatter_sums.1 = f32[2,512,256]{2,1,0:T(8,128)} custom-call(f32[8,512,256]{2,1,0:T(8,128)} %get-tuple-element.8.col_ref, f32[16,512,256]{2,1,0:T(8,128)} %get-tuple-element.9.row_ref), custom_call_target="tpu_custom_call" | custom-call | tf_op jit(solution)/shard_map/scatter_sums/pallas_call | solution.py:383
  197.3 0.0 copy-start
  197.4 2.2 convolution_bitcast_fusion
  199.6 3.5 %convolution_bitcast_fusion.1 = f32[256,256]{1,0:T(8,128)S(1)} fusion(f32[2,512,256]{2,1,0:T(8,128)} %scatter_sums.1), kind=kOutput, calls=%fused_computation.3 | convolution fusion | flops 805306368 | bytes 1310720 | tf_op jit(solution)/shard_map/dot_general | solution.py:510
  203.0 0.8 pad_maximum_fusion
  203.9 28.0 %sum_all.2 = f32[4,8,16,256]{3,2,1,0:T(8,128)} custom-call(f32[4,8,16,256]{3,2,1,0:T(8,128)} %bitcast.42), custom_call_target="tpu_custom_call" | custom-call | tf_op jit(solution)/shard_map/sum_all/pallas_call | solution.py:155
  231.9 1.9 slice_multiply_fusion
  233.8 14.7 %inverse_factor.2 = f32[256,256]{1,0:T(8,128)} custom-call(f32[256,256]{1,0:T(8,128)} %bitcast.45), custom_call_target="tpu_custom_call" | custom-call | tf_op jit(solution)/shard_map/inverse_factor/pallas_call | solution.py:496
  248.4 0.0 copy-done
  248.4 2.0 fusion.2
  250.4 2.5 fusion.3
  252.9 21.3 %sum_all.3 = f32[4,8,8,256]{3,2,1,0:T(8,128)} custom-call(f32[4,8,8,256]{3,2,1,0:T(8,128)} %bitcast.43), custom_call_target="tpu_custom_call" | custom-call | tf_op jit(solution)/shard_map/sum_all/pallas_call | solution.py:155
  274.2 4.7 %inverse_factor.3 = f32[256,256]{1,0:T(8,128)} custom-call(f32[256,256]{1,0:T(8,128)} %bitcast.44), custom_call_target="tpu_custom_call" | custom-call | tf_op jit(solution)/shard_map/inverse_factor/pallas_call | solution.py:496
  278.9 2.8 fusion
Async XLA Ops:
  197.3 51.1 %copy-start = (f32[2,512,256]{2,1,0:T(8,128)S(1)}, f32[2,512,256]{2,1,0:T(8,128)}, u32[]{:S(2)}) copy-start(f32[2,512,256]{2,1,0:T(8,128)} %scatter_sums.1) | copy-start | bytes 3145732

commit v4 on v3

--- a/solution.py
+++ b/solution.py
@@ -349,20 +349,22 @@
                 copy = sender.start(
                     mid.at[s - 1, b], land_out.at[s - 1, b], side.device(s, 0)
                 )
-                arrivals.append((mid, land_out, s, b, side, copy))
-    for mid, land_out, s, b, side, copy in arrivals:
+                arrivals.append((land_out, (s, b), copy))
+    for _, _, copy in arrivals:
         copy.wait_recv()
-        add_into(mid.at[side.outer_count - 1, b], land_out.at[s - 1, b])
-    col_mid, row_mid = plans[0][1], plans[1][1]
-    col_last, row_last = plans[0][0].outer_count - 1, plans[1][0].outer_count - 1
     edge = out_ref.shape[1]
     step = min(64, edge)
     for b in range(own):
+        terms = [mid.at[side.outer_count - 1, b] for side, mid, _, _, _ in plans]
+        terms += [land_out.at[s - 1, b] for land_out, (s, block), _ in arrivals if block == b]
 
         @pl.loop(0, edge // step)
         def _(i):
             part = pl.ds(pl.multiple_of(i * step, step), step)
-            out_ref[b, part, :] = col_mid[col_last, b, part, :] + row_mid[row_last, b, part, :]
+            total = terms[0][part, :]
+            for term in terms[1:]:
+                total += term[part, :]
+            out_ref[b, part, :] = total
 
     sender.finish()
 
@@ -403,7 +405,7 @@
     rows = lax.broadcasted_iota(jnp.int32, (n, n), 0)
     cols = lax.broadcasted_iota(jnp.int32, (n, n), 1)
     pivots = jnp.ones((n, n), jnp.float32)
-    group = 4
+    group = 8
     for start in range(0, n, group):
         members = range(start, start + group)
         columns = {j: jnp.broadcast_to(x[:, j : j + 1], (n, n)) for j in members}
@@ -535,9 +537,9 @@
     )
     product = scatter_sums(col_partial, row_partial, own_blocks).reshape(own_blocks * edge, rank)
     old = basis.reshape(own_blocks * edge, rank).astype(jnp.float32)
-    sums = sum_all(jnp.concatenate([gram_of(product, product), gram_of(old, product)], 0), 0)
+    sums = sum_all(gram_of(jnp.concatenate([product, old / scale], 1), product), 0)
     gram = sums[:rank]
-    projected = sums[rank:] / scale
+    projected = sums[rank:]
     first_basis = times_transposed(product, inverse_factor(gram))
     second = sum_all(gram_of(first_basis, first_basis), 1)
     final = times_transposed(first_basis, inverse_factor(second, near_identity=True))

time: 283 us -> 281 us (level)
  local copies, waits for them, and re-layouts: 0.01 us -> 3.92 us
  matrix products: 13 us -> 9.87 us
    dot_general x3 -> x2, matrix products: 8.22 us -> 5.14 us  [gram_of(): return lax.dot_general(x, y, (((0,), (0,)), ((), ())), precision=HIGHEST)]
where the time goes in v4:
time: 281 us; the launch traced here: 282 us
  Pallas kernels  263 us (94%)
  matrix products  9.87 us (4%)
  other arithmetic  4.96 us (2%)
  local copies, waits for them, and re-layouts  3.92 us (1%)
    pallas_call x1, Pallas kernels, scatter_sums(): pl.pallas_call(functools.partial(scatter_kernel, nr, nc, own), out_shape=...  118 us
    pallas_call x1, Pallas kernels, gather_sides(): pl.pallas_call(functools.partial(gather_kernel, nr, nc, own), out_shape=[...  57 us
    pallas_call x2, Pallas kernels, sum_all(): pl.pallas_call(functools.partial(sum_kernel, nr, nc), out_shape=jax.Shape...  51.7 us
    pallas_call x1, Pallas kernels, tile_products(): pl.pallas_call(tile_kernel, grid_spec=pltpu.PrefetchScalarGridSpec(num_sc...  18.6 us
    pallas_call x2, Pallas kernels, inverse_factor(): pl.pallas_call(functools.partial(inverse_kernel, 32, near_identity), out_...  17.4 us

profile of v4, /device:TPU:1, one launch (start us, length us, event | category | flops | bytes accessed | tf_op | source)
XLA Modules:
  0.0 282.3 jit_solution(10805984010378100255)
XLA Ops:
  0.6 57.0 %gather_sides.1 = (bf16[8,512,256]{2,1,0:T(8,128)(2,1)}, bf16[16,512,256]{2,1,0:T(8,128)(2,1)}) custom-call(bf16[2,512,256]{2,1,0:T(8,128)(2,1)} %own_ref.1), custom_call_target="tpu_custom_call" | custom-call | tf_op jit(solution)/shard_map/gather_sides/pallas_call | solution.py:285
  57.6 0.9 select_reduce_fusion
  58.5 1.2 bitcast_select_fusion
  59.7 18.6 %tile_products.1 = (f32[16,512,256]{2,1,0:T(8,128)}, f32[8,512,256]{2,1,0:T(8,128)}) custom-call(s32[16]{0:T(128)} %get-tuple-element.13.row_local, s32[16]{0:T(128)} %get-tuple-element.12.col_local, bf16[16,512,512]{2,1,0:T(8,128)(2,1)} %tile_ref.1, bf16[8,512,256]{2,1,0:T(8,128)(2,1)} %get-tuple-element.6.col_side, ...), custom_call_target="tpu_custom_call" | custom-call | tf_op jit(solution)/shard_map/tile_products/pallas_call | solution.py:50
  78.3 118.2 %scatter_sums.1 = f32[2,512,256]{2,1,0:T(8,128)} custom-call(f32[8,512,256]{2,1,0:T(8,128)} %get-tuple-element.8.col_ref, f32[16,512,256]{2,1,0:T(8,128)} %get-tuple-element.9.row_ref), custom_call_target="tpu_custom_call" | custom-call | tf_op jit(solution)/shard_map/scatter_sums/pallas_call | solution.py:385
  196.5 0.0 copy-start
  196.5 1.2 convert_multiply_fusion
  197.8 0.1 copy-done
  197.9 1.7 maximum_bitcast_fusion
  199.6 1.9 copy.8
  201.5 2.6 fusion.3.x_ref
  204.1 30.9 %sum_all.2 = f32[4,8,16,256]{3,2,1,0:T(8,128)} custom-call(f32[4,8,16,256]{3,2,1,0:T(8,128)} %fusion.3.x_ref), custom_call_target="tpu_custom_call" | custom-call | tf_op jit(solution)/shard_map/sum_all/pallas_call | solution.py:155
  235.0 1.9 fusion.2
  236.9 12.7 %inverse_factor.2 = f32[256,256]{1,0:T(8,128)} custom-call(f32[256,256]{1,0:T(8,128)} %bitcast.47), custom_call_target="tpu_custom_call" | custom-call | tf_op jit(solution)/shard_map/inverse_factor/pallas_call | solution.py:498
  249.5 2.0 fusion.4
  251.5 2.5 fusion.5
  254.0 20.8 %sum_all.3 = f32[4,8,8,256]{3,2,1,0:T(8,128)} custom-call(f32[4,8,8,256]{3,2,1,0:T(8,128)} %bitcast.45), custom_call_target="tpu_custom_call" | custom-call | tf_op jit(solution)/shard_map/sum_all/pallas_call | solution.py:155
  274.8 4.7 %inverse_factor.3 = f32[256,256]{1,0:T(8,128)} custom-call(f32[256,256]{1,0:T(8,128)} %bitcast.46), custom_call_target="tpu_custom_call" | custom-call | tf_op jit(solution)/shard_map/inverse_factor/pallas_call | solution.py:498
  279.5 2.8 fusion
Async XLA Ops:
  196.5 1.4 copy-start
